TPU v7x, 128 devices: a whole 4x4x4 slice. The times are simulated.
128 devices in a mesh: req: 32 (over x, y, core), mlp: 4 (over z).
Axes of the slice: x: 4, y: 4, z: 4, core: 2. Of those that a mesh axis runs over, the one named last changes fastest.
Arguments:
- tokens: bfloat16 [1024, 2048], P('req'), may hold values from -6 to 6
- prefix_len: int32 [32], replicated, may hold values from 1 to 4096, 65536 in all
- tail_len: int32 [32, 16], replicated, may hold values from 1 to 64, 512 in all within a row
- tail_src: int32 [512], replicated, may hold values from 0 to 31, as said below
- prefix_kv: bfloat16 [32, 2, 4096, 2048], P('req', None, None, 'mlp'), may hold values from -256 to 256, as said below
- tail_kv: bfloat16 [512, 2, 64, 2048], P('req', None, None, 'mlp'), may hold values from -256 to 256, as said below
- w_qkv: bfloat16 [2048, 3, 2048], P(None, None, 'mlp'), may hold values from -0.125 to 0.125
- w_out: bfloat16 [2048, 2048], P('mlp'), may hold values from -0.125 to 0.125
- w_gate: bfloat16 [8192, 2048], P(('req', 'mlp')), may hold values from -0.125 to 0.125
- w_up: bfloat16 [8192, 2048], P(('req', 'mlp')), may hold values from -0.125 to 0.125
- w_down: bfloat16 [8192, 2048], P(('req', 'mlp')), may hold values from -0.0625 to 0.0625
- w_score: float32 [2048], replicated, may hold values from -0.125 to 0.125
Outputs:
- layer_out: bfloat16 [1024, 2048], P(('req', 'mlp'))
- score: float32 [1024], P(('req', 'mlp'))
Inputs may be any that keep to these rules, and one draw needn't show every extreme that they name: tail_src[c] is the req index whose shard of tail_kv holds the tail of continuation c; each device holds 16 tails, in increasing order of continuation. The 16 continuations of a prompt come in groups of 1 from 16 different devices, so from one device to the device of one prompt goes exactly one tail or none. `prefix_kv`: keys are already rotated. `tail_kv`: keys are already rotated.
All inputs are finite; a program needn't handle non-finite values.
Results may differ from a plain program's by a relative error of at most 0.027.
Values may be sent and summed in bfloat16 or wider, within the bound.
A program may use at most 128 MiB of HBM per device.

v0:
```python
from functools import reduce
import jax
import jax.numpy as jnp
from jax import lax
from jax.sharding import PartitionSpec as P

HEAD_DIM = 128
CONT = 16
NEW = 2


def layer_norm(values):
    centre = values - jnp.mean(values, axis=-1, keepdims=True)
    spread = jnp.mean(centre * centre, axis=-1, keepdims=True)
    return centre * lax.rsqrt(spread + 1e-05)


def rotate(vectors, positions):
    half_dim = vectors.shape[-1] // 2
    exponent = jnp.arange(half_dim, dtype=jnp.float32) * (2.0 / vectors.shape[-1])
    frequency = jnp.power(10000.0, -exponent)
    phase_radians = positions.astype(jnp.float32)[:, None] * frequency[None, :]
    cosine = jnp.cos(phase_radians)[:, None, :]
    sine_part = jnp.sin(phase_radians)[:, None, :]
    leading = vectors[..., :half_dim]
    trailing = vectors[..., half_dim:]
    return jnp.concatenate(
        [leading * cosine - trailing * sine_part, trailing * cosine + leading * sine_part], axis=-1
    )


def attend(queries, key_rows, values, key_mask):
    scaling = queries.shape[-1] ** (-0.5)
    scores = (
        jnp.einsum("cjhe,ckhe->cjhk", queries, key_rows, preferred_element_type=jnp.float32)
        * scaling
    )
    scores = jnp.where(key_mask, scores, -1e30)
    row_max = jnp.max(scores, axis=-1)
    weights = jnp.where(key_mask, jnp.exp(scores - row_max[..., None]), 0.0)
    row_sum = jnp.sum(weights, axis=-1)
    output = jnp.einsum(
        "cjhk,ckhe->cjhe", weights.astype(jnp.bfloat16), values, preferred_element_type=jnp.float32
    )
    return (row_max, row_sum, output)


def tail_attend(queries, cache_rows, lengths):
    local_heads = queries.shape[2]
    shaped = (cache_rows.shape[0], cache_rows.shape[2], local_heads, HEAD_DIM)
    key_rows = cache_rows[:, 0].reshape(shaped)
    value_rows = cache_rows[:, 1].reshape(shaped)
    tail_mask = (jnp.arange(cache_rows.shape[2], dtype=jnp.int32)[None, :] < lengths[:, None])[
        :, None, None, :
    ]
    return attend(queries, key_rows, value_rows, tail_mask)


def combine(pieces):
    overall = reduce(jnp.maximum, [piece[0] for piece in pieces])
    numerator = jnp.zeros_like(pieces[0][2])
    denominator = jnp.zeros_like(pieces[0][1])
    for piece in pieces:
        scale_factor = jnp.exp(piece[0] - overall)
        numerator = numerator + scale_factor[..., None] * piece[2]
        denominator = denominator + scale_factor * piece[1]
    return numerator / denominator[..., None]


def swiglu(normed, gate_rows, up_rows, down_rows):
    contract = (((1,), (1,)), ((), ()))
    gate_out = lax.dot_general(normed, gate_rows, contract, preferred_element_type=jnp.float32)
    up_out = lax.dot_general(normed, up_rows, contract, preferred_element_type=jnp.float32)
    hidden = (jax.nn.silu(gate_out) * up_out).astype(jnp.bfloat16)
    return jnp.dot(hidden, down_rows, preferred_element_type=jnp.float32)


def on_device(
    tokens,
    prefix_len,
    tail_len,
    tail_src,
    prefix_kv,
    tail_kv,
    w_qkv,
    w_out,
    w_gate,
    w_up,
    w_down,
    w_score,
):
    req_index = lax.axis_index("req")
    req_count = lax.axis_size("req")
    cap_rows = max(1, CONT // req_count)
    tok_count = tokens.shape[0]
    head_width = w_qkv.shape[2]
    local_heads = head_width // HEAD_DIM
    prefix_size = prefix_kv.shape[2]
    grouped = (CONT, NEW, local_heads, HEAD_DIM)
    normed = layer_norm(tokens.astype(jnp.float32)).astype(jnp.bfloat16)
    projected = jnp.einsum("td,dcf->tcf", normed, w_qkv, preferred_element_type=jnp.float32)
    own_prefix = lax.dynamic_index_in_dim(prefix_len, req_index, 0, keepdims=False)
    own_tails = lax.dynamic_index_in_dim(tail_len, req_index, 0, keepdims=False)
    offsets = jnp.arange(NEW, dtype=jnp.int32)
    positions = (own_prefix + own_tails[:, None] + offsets[None, :]).reshape(-1)
    queries = rotate(projected[:, 0].reshape(tok_count, local_heads, HEAD_DIM), positions).astype(
        jnp.bfloat16
    )
    new_keys = rotate(projected[:, 1].reshape(tok_count, local_heads, HEAD_DIM), positions).astype(
        jnp.bfloat16
    )
    new_values = projected[:, 2].astype(jnp.bfloat16)
    prefix_keys = prefix_kv[0, 0].reshape(1, prefix_size, local_heads, HEAD_DIM)
    prefix_values = prefix_kv[0, 1].reshape(1, prefix_size, local_heads, HEAD_DIM)
    prefix_mask = (jnp.arange(prefix_size, dtype=jnp.int32) < own_prefix)[None, None, None, :]
    prefix_part = attend(
        queries.reshape(1, tok_count, local_heads, HEAD_DIM),
        prefix_keys,
        prefix_values,
        prefix_mask,
    )
    prefix_part = tuple((member.reshape((CONT, NEW) + member.shape[2:]) for member in prefix_part))
    conts_all = tail_src.shape[0]
    indices = jnp.arange(conts_all, dtype=jnp.int32)
    owners = indices // CONT
    paired = (
        (tail_src[None, :] == tail_src[:, None])
        & (owners[None, :] == owners[:, None])
        & (indices[None, :] < indices[:, None])
    )
    pair_rank = jnp.sum(paired.astype(jnp.int32), axis=1)
    held_ids = jnp.nonzero(tail_src == req_index, size=CONT)[0].astype(jnp.int32)
    send_slots = owners[held_ids] * cap_rows + pair_rank[held_ids]
    own_ids = req_index * CONT + jnp.arange(CONT, dtype=jnp.int32)
    recv_slots = tail_src[own_ids] * cap_rows + pair_rank[own_ids]
    slots_total = req_count * cap_rows
    outgoing = (
        jnp.zeros((slots_total,) + tail_kv.shape[1:], jnp.bfloat16).at[send_slots].set(tail_kv)
    )
    incoming = lax.all_to_all(outgoing, "req", split_axis=0, concat_axis=0, tiled=True)
    fetched = incoming[recv_slots]
    tail_part = tail_attend(queries.reshape(grouped), fetched, own_tails)
    new_mask = (offsets[:, None] >= offsets[None, :])[None, :, None, :]
    new_part = attend(
        queries.reshape(grouped), new_keys.reshape(grouped), new_values.reshape(grouped), new_mask
    )
    attn_mix = (
        combine([prefix_part, tail_part, new_part])
        .reshape(tok_count, head_width)
        .astype(jnp.bfloat16)
    )
    partial_value = jnp.dot(attn_mix, w_out, preferred_element_type=jnp.float32)
    summed = lax.psum(partial_value, "mlp")
    residual = (tokens.astype(jnp.float32) + summed).astype(jnp.bfloat16)
    normed_mid = layer_norm(residual.astype(jnp.float32)).astype(jnp.bfloat16)
    row_share = tok_count // lax.axis_size("mlp")
    mlp_index = lax.axis_index("mlp")
    collected_entries = lax.all_gather(normed_mid, "req", axis=0, tiled=True)
    mlp_sum = lax.psum_scatter(
        swiglu(collected_entries, w_gate, w_up, w_down),
        ("req", "mlp"),
        scatter_dimension=0,
        tiled=True,
    )
    own_rows = lax.dynamic_slice_in_dim(residual, mlp_index * row_share, row_share, 0)
    layer_f32 = own_rows.astype(jnp.float32) + mlp_sum
    layer_out = layer_f32.astype(jnp.bfloat16)
    score = jnp.sum(layer_norm(layer_f32) * w_score[None, :], axis=-1)
    return (layer_out, score)


def solution(mesh):
    in_specs = (
        P("req", None),
        P(),
        P(),
        P(),
        P("req", None, None, "mlp"),
        P("req", None, None, "mlp"),
        P(None, None, "mlp"),
        P("mlp", None),
        P(("req", "mlp"), None),
        P(("req", "mlp"), None),
        P(("req", "mlp"), None),
        P(),
    )
    out_specs = (P(("req", "mlp"), None), P(("req", "mlp")))
    return jax.shard_map(
        on_device, mesh=mesh, in_specs=in_specs, out_specs=out_specs, check_vma=False
    )
```

profile of v0, /device:TPU:0, one launch (start us, length us, event | category | flops | bytes accessed | tf_op | source)
XLA Modules:
  0.0 868.8 jit_solution(6250330086719967981)
XLA Ops:
  7.2 1.5 convert_reduce_fusion.3
  8.7 1.1 convert_reduce_fusion
  9.7 0.3 reduce-window.12
  10.4 4.1 scatter_custom_fusion
  14.6 0.8 fusion.58
  15.3 0.7 gather_fusion
  16.0 0.7 gather_fusion.1
  16.9 2.4 broadcast_in_dim.121
  19.3 6.0 scatter_fusion
  25.3 7.7 all-to-all-start
  33.2 0.7 gather_fusion.3
  33.8 0.7 gather_fusion.2
  34.5 0.6 dynamic_slice.11
  35.4 0.2 fusion.23
  35.6 0.7 broadcast_add_fusion.1
  36.5 4.0 fusion.34
  41.2 0.3 fusion.50
  41.6 0.7 fusion.67
  42.5 5.7 fusion.78
  48.2 6.4 copy.222
  54.6 0.7 iota_compare_fusion.1
  55.3 4.4 fusion.84
  59.7 2.1 fusion.3
  62.1 6.4 copy.225
  69.0 4.4 fusion.10
  73.4 12.4 %all-to-all-done = bf16[32,2,64,512]{3,2,1,0:T(8,128)(2,1)} async-done(((bf16[32,2,64,512]{3,2,1,0:T(8,128)(2,1)}), bf16[32,2,64,512]{3,2,1,0:T(8,128)(2,1)}, u32[]{:S(2)}, u32[]{:S(2)}) %all-to-all-start) | async-done | bytes 4194336 | tf_op jit(solution)/shard_map/all_to_all | solution.py:140
  85.7 4.2 gather_fusion.4
  90.0 2.7 fusion.79
  92.7 2.2 reshape_squeeze.15
  94.9 2.0 fusion.83
  96.9 0.9 fusion.66
  97.9 0.7 copy.210
  98.6 1.1 reshape_squeeze.17
  99.7 1.7 fusion.12
  101.4 0.7 multiply_add_fusion
  102.3 1.2 fusion.43
  103.6 43.6 %all-reduce.2.cloned.1.call-done = f32[32,2048]{1,0:T(8,128)} async-done(((f32[32,2048]{1,0:T(8,128)}), f32[32,2048]{1,0:T(8,128)}) %all-reduce.2.cloned.1.call-update) | async-done | bytes 262160 | tf_op jit(solution)/shard_map/psum | solution.py:153
  147.1 1.1 convert_reduce_fusion.2
  148.2 0.2 fusion.25
  148.4 0.7 fusion.26
  149.2 0.2 reduce-scatter.2.cloned.1.call-start
  149.4 46.5 %all-gather.2.cloned.1.call-done = bf16[1024,2048]{1,0:T(8,128)(2,1)} async-done(((bf16[32,2048]{1,0:T(8,128)(2,1)}), bf16[1024,2048]{1,0:T(8,128)(2,1)}) %all-gather.2.cloned.1.call-update) | async-done | bytes 4194320 | tf_op jit(solution)/shard_map/all_gather | solution.py:158
  195.9 3.6 fusion.85
  199.5 8.0 fusion.6
  207.5 650.6 %reduce-scatter.2.cloned.1.call-done = f32[8,2048]{1,0:T(8,128)} async-done(((f32[1024,2048]{1,0:T(8,128)}), f32[8,2048]{1,0:T(8,128)}) %reduce-scatter.2.cloned.1.call-update) | async-done | bytes 65552 | tf_op jit(solution)/shard_map/reduce_scatter | solution.py:159
  858.1 1.0 fusion.75
  859.1 1.0 multiply_reduce_fusion.1
  860.2 2.1 multiply_reduce_fusion
  (78 shorter events, 3.5 us)
Async XLA Ops:
  7.2 95.1 %copy-start = (bf16[512,2048]{1,0:T(8,128)(2,1)S(1)}, bf16[512,2048]{1,0:T(8,128)(2,1)}, u32[]{:S(2)}) copy-start(bf16[512,2048]{1,0:T(8,128)(2,1)} %param.19) | copy-start | bytes 6291460
  25.3 8.5 copy-start.1
  25.3 9.2 %copy-start.9 = (s32[32]{0:T(128)S(1)}, s32[32]{0:T(128)}, u32[]{:S(2)}) copy-start(s32[32]{0:T(128)} %param.13) | copy-start | bytes 388
  25.3 9.8 %copy-start.8 = (s32[32,16]{0,1:T(8,128)S(1)}, s32[32,16]{0,1:T(8,128)}, u32[]{:S(2)}) copy-start(s32[32,16]{0,1:T(8,128)} %param.14) | copy-start | bytes 6148
  25.3 10.0 %copy-start.2 = (bf16[32,2048]{1,0:T(8,128)(2,1)S(1)}, bf16[32,2048]{1,0:T(8,128)(2,1)}, u32[]{:S(2)}) copy-start(bf16[32,2048]{1,0:T(8,128)(2,1)} %param.12) | copy-start | bytes 393220
  25.3 60.4 %all-to-all-start = ((bf16[32,2,64,512]{3,2,1,0:T(8,128)(2,1)}), bf16[32,2,64,512]{3,2,1,0:T(8,128)(2,1)}, u32[]{:S(2)}, u32[]{:S(2)}) async-start(bf16[32,2,64,512]{3,2,1,0:T(8,128)(2,1)} %scatter_fusion), calls=%async_computation | async-start | bytes 8388608 | tf_op jit(solution)/shard_map/all_to_all | solution.py:140
  33.0 114.2 %all-reduce.2.cloned.1.call-start = ((), (), s32[]{:S(2)}) async-start(), calls=%async_computation.2 | async-start | bytes 524288 | tf_op jit(solution)/shard_map/psum | solution.py:153
  68.8 26.1 %copy-start.6 = (pred[16,64]{1,0:T(8,128)(4,1)}, pred[16,64]{1,0:T(8,128)(4,1)S(1)}, u32[]{:S(2)}) copy-start(pred[16,64]{1,0:T(8,128)(4,1)S(1)} %iota_compare_fusion.3) | copy-start | bytes 3076
  99.7 96.2 %copy-start.3 = (bf16[64,2048]{1,0:T(8,128)(2,1)S(1)}, bf16[64,2048]{1,0:T(8,128)(2,1)}, u32[]{:S(2)}) copy-start(bf16[64,2048]{1,0:T(8,128)(2,1)} %param.20) | copy-start | bytes 786436
  102.3 97.2 %copy-start.4 = (bf16[64,2048]{1,0:T(8,128)(2,1)S(1)}, bf16[64,2048]{1,0:T(8,128)(2,1)}, u32[]{:S(2)}) copy-start(bf16[64,2048]{1,0:T(8,128)(2,1)} %param.22) | copy-start | bytes 786436
  102.3 97.2 %copy-start.5 = (bf16[64,2048]{1,0:T(8,128)(2,1)S(1)}, bf16[64,2048]{1,0:T(8,128)(2,1)}, u32[]{:S(2)}) copy-start(bf16[64,2048]{1,0:T(8,128)(2,1)} %param.21) | copy-start | bytes 786436
  103.5 92.4 %all-gather.2.cloned.1.call-start = ((), (), s32[]{:S(2)}) async-start(), calls=%async_computation.3 | async-start | bytes 4325376 | tf_op jit(solution)/shard_map/all_gather | solution.py:158
  149.2 708.9 %reduce-scatter.2.cloned.1.call-start = ((), (), s32[]{:S(2)}) async-start(), calls=%async_computation.4 | async-start | bytes 8454144 | tf_op jit(solution)/shard_map/reduce_scatter | solution.py:159
  207.5 652.7 %copy-start.7 = (f32[2048]{0:T(1024)S(1)}, f32[2048]{0:T(1024)}, u32[]{:S(2)}) copy-start(f32[2048]{0:T(1024)} %param.23) | copy-start | bytes 24580
Sparse Core Ops, SparseCore 0:
  103.6 43.4 all-reduce.1
  149.6 46.2 all-gather.1
  207.6 650.4 reduce-scatter.1
where the time goes:
time: 870 us; the launch traced here: 869 us
  waiting for transfers between devices  753 us (87%)
  local copies, waits for them, and re-layouts  42.9 us (5%)
  matrix products  29.6 us (3%)
  other arithmetic  21.2 us (2%)
  between operations  14 us (2%)
    reduce_scatter x1, waiting for transfers between devices, on_device(): lax.psum_scatter(swiglu(collected_entries, w_gate, w_up, w_down), ('req',...  651 us
    all_gather x1, waiting for transfers between devices, on_device(): collected_entries = lax.all_gather(normed_mid, 'req', axis=0, tiled=True)  46.5 us
    psum x1, waiting for transfers between devices, on_device(): summed = lax.psum(partial_value, 'mlp')  43.6 us
  transfers between devices with their start and end apart: 4, of which 4 were waited for; matrix products, arithmetic and copies ran while one was open for 5% of the time, Pallas kernels for 0%

commit v1 on v0

--- a/solution.py
+++ b/solution.py
@@ -1,3 +1,4 @@
+import functools
 from functools import reduce
 import jax
 import jax.numpy as jnp
@@ -7,6 +8,22 @@
 HEAD_DIM = 128
 CONT = 16
 NEW = 2
+
+
+def find_waves(incoming_x, named_axis):
+    shares = lax.axis_size(named_axis)
+    left_arr, upper = (incoming_x, 0)
+    while 1 << upper < shares:
+        top = range(shares)
+        state_now = map(lambda dd: (dd, dd ^ 1 << upper), top)
+        extra = list(state_now)
+        state_next = lax.ppermute(left_arr, axis_name=named_axis, perm=extra)
+        left_arr = left_arr + state_next
+        upper = upper + 1
+    return left_arr
+
+
+lead_sources_all_here = functools.partial(find_waves, named_axis="mlp")
 
 
 def layer_norm(values):
@@ -150,7 +167,7 @@
         .astype(jnp.bfloat16)
     )
     partial_value = jnp.dot(attn_mix, w_out, preferred_element_type=jnp.float32)
-    summed = lax.psum(partial_value, "mlp")
+    summed = lead_sources_all_here(partial_value)
     residual = (tokens.astype(jnp.float32) + summed).astype(jnp.bfloat16)
     normed_mid = layer_norm(residual.astype(jnp.float32)).astype(jnp.bfloat16)
     row_share = tok_count // lax.axis_size("mlp")

time: 870 us -> 843 us (0.969)
  waiting for transfers between devices: 753 us -> 722 us
    psum x1 -> x0, waiting for transfers between devices: 43.6 us -> none  [on_device(): summed = lax.psum(partial_value, 'mlp')]
    ppermute x0 -> x2, waiting for transfers between devices: none -> 11.3 us  [find_waves(): state_next = lax.ppermute(left_arr, axis_name=named_axis, perm=extra)]
  transfers between devices with their start and end apart: 4 -> 5, of which waited for: 4 -> 5; matrix products, arithmetic and copies ran while one was open for 5% -> 5% of each run, Pallas kernels for 0% -> 0%
where the time goes in v1:
time: 843 us; the launch traced here: 842 us
  waiting for transfers between devices  722 us (86%)
  local copies, waits for them, and re-layouts  42.9 us (5%)
  matrix products  28.9 us (3%)
  other arithmetic  20.4 us (2%)
  between operations  14.3 us (2%)
  starting transfers between devices  13.7 us (2%)
    reduce_scatter x1, waiting for transfers between devices, on_device(): lax.psum_scatter(swiglu(collected_entries, w_gate, w_up, w_down), ('req',...  652 us
    all_gather x1, waiting for transfers between devices, on_device(): collected_entries = lax.all_gather(normed_mid, 'req', axis=0, tiled=True)  46.8 us
  transfers between devices with their start and end apart: 5, of which 5 were waited for; matrix products, arithmetic and copies ran while one was open for 5% of the time, Pallas kernels for 0%

profile of v1, /device:TPU:0, one launch (start us, length us, event | category | flops | bytes accessed | tf_op | source)
XLA Modules:
  0.0 842.2 jit_solution(12766358479816505497)
XLA Ops:
  7.2 1.5 convert_reduce_fusion.3
  8.7 1.1 convert_reduce_fusion
  9.7 0.3 reduce-window.12
  10.4 4.1 scatter_custom_fusion
  14.6 0.8 fusion.58
  15.3 0.7 gather_fusion
  16.0 0.7 gather_fusion.1
  16.9 2.4 broadcast_in_dim.121
  19.3 6.0 scatter_fusion
  25.3 7.7 all-to-all-start
  33.2 0.7 gather_fusion.3
  33.8 0.7 gather_fusion.2
  34.5 0.6 dynamic_slice.11
  35.6 0.7 broadcast_add_fusion.1
  36.5 4.0 fusion.34
  41.2 0.3 fusion.50
  41.6 0.7 fusion.67
  42.5 5.7 fusion.78
  48.2 6.4 copy.222
  54.6 0.7 iota_compare_fusion.1
  55.3 4.4 fusion.84
  59.7 2.1 fusion.3
  62.1 6.4 copy.225
  69.0 4.4 fusion.10
  73.4 12.4 %all-to-all-done = bf16[32,2,64,512]{3,2,1,0:T(8,128)(2,1)} async-done(((bf16[32,2,64,512]{3,2,1,0:T(8,128)(2,1)}), bf16[32,2,64,512]{3,2,1,0:T(8,128)(2,1)}, u32[]{:S(2)}, u32[]{:S(2)}) %all-to-all-start) | async-done | bytes 4194336 | tf_op jit(solution)/shard_map/all_to_all | solution.py:157
  85.7 4.2 gather_fusion.4
  90.0 2.7 fusion.79
  92.7 2.2 reshape_squeeze.15
  94.9 2.0 fusion.83
  96.9 0.9 fusion.66
  97.9 0.7 copy.210
  98.6 1.1 reshape_squeeze.17
  99.7 1.7 fusion.12
  101.4 0.7 multiply_add_fusion
  102.3 0.5 fusion.43
  102.8 2.0 collective-permute-start
  104.8 6.1 collective-permute-done
  110.9 3.8 collective-permute-start.1
  114.7 5.2 collective-permute-done.1
  120.3 0.7 fusion.26
  121.1 0.2 reduce-scatter.2.cloned.1.call-start
  121.3 46.8 %all-gather.2.cloned.1.call-done = bf16[1024,2048]{1,0:T(8,128)(2,1)} async-done(((bf16[32,2048]{1,0:T(8,128)(2,1)}), bf16[1024,2048]{1,0:T(8,128)(2,1)}) %all-gather.2.cloned.1.call-update) | async-done | bytes 4194320 | tf_op jit(solution)/shard_map/all_gather | solution.py:175
  168.1 3.6 fusion.85
  171.7 8.0 fusion.6
  179.7 651.6 %reduce-scatter.2.cloned.1.call-done = f32[8,2048]{1,0:T(8,128)} async-done(((f32[1024,2048]{1,0:T(8,128)}), f32[8,2048]{1,0:T(8,128)}) %reduce-scatter.2.cloned.1.call-update) | async-done | bytes 65552 | tf_op jit(solution)/shard_map/reduce_scatter | solution.py:176
  831.2 1.0 fusion.75
  832.2 1.0 multiply_reduce_fusion.1
  833.3 2.1 multiply_reduce_fusion
  (80 shorter events, 4.0 us)
Async XLA Ops:
  7.2 95.1 %copy-start = (bf16[512,2048]{1,0:T(8,128)(2,1)S(1)}, bf16[512,2048]{1,0:T(8,128)(2,1)}, u32[]{:S(2)}) copy-start(bf16[512,2048]{1,0:T(8,128)(2,1)} %param.19) | copy-start | bytes 6291460
  25.3 8.5 %copy-start.1 = (s32[512]{0:T(512)S(1)}, s32[512]{0:T(512)}, u32[]{:S(2)}) copy-start(s32[512]{0:T(512)} %param.15) | copy-start | bytes 6148
  25.3 9.2 %copy-start.9 = (s32[32]{0:T(128)S(1)}, s32[32]{0:T(128)}, u32[]{:S(2)}) copy-start(s32[32]{0:T(128)} %param.13) | copy-start | bytes 388
  25.3 9.8 %copy-start.8 = (s32[32,16]{0,1:T(8,128)S(1)}, s32[32,16]{0,1:T(8,128)}, u32[]{:S(2)}) copy-start(s32[32,16]{0,1:T(8,128)} %param.14) | copy-start | bytes 6148
  25.3 10.0 %copy-start.2 = (bf16[32,2048]{1,0:T(8,128)(2,1)S(1)}, bf16[32,2048]{1,0:T(8,128)(2,1)}, u32[]{:S(2)}) copy-start(bf16[32,2048]{1,0:T(8,128)(2,1)} %param.12) | copy-start | bytes 393220
  25.3 60.4 %all-to-all-start = ((bf16[32,2,64,512]{3,2,1,0:T(8,128)(2,1)}), bf16[32,2,64,512]{3,2,1,0:T(8,128)(2,1)}, u32[]{:S(2)}, u32[]{:S(2)}) async-start(bf16[32,2,64,512]{3,2,1,0:T(8,128)(2,1)} %scatter_fusion), calls=%async_computation | async-start | bytes 8388608 | tf_op jit(solution)/shard_map/all_to_all | solution.py:157
  33.0 135.1 %all-gather.2.cloned.1.call-start = ((), (), s32[]{:S(2)}) async-start(), calls=%async_computation.2 | async-start | bytes 4325376 | tf_op jit(solution)/shard_map/all_gather | solution.py:175
  68.8 26.1 %copy-start.6 = (pred[16,64]{1,0:T(8,128)(4,1)}, pred[16,64]{1,0:T(8,128)(4,1)S(1)}, u32[]{:S(2)}) copy-start(pred[16,64]{1,0:T(8,128)(4,1)S(1)} %iota_compare_fusion.3) | copy-start | bytes 3076
  99.7 68.4 %copy-start.3 = (bf16[64,2048]{1,0:T(8,128)(2,1)S(1)}, bf16[64,2048]{1,0:T(8,128)(2,1)}, u32[]{:S(2)}) copy-start(bf16[64,2048]{1,0:T(8,128)(2,1)} %param.20) | copy-start | bytes 786436
  102.8 68.9 %copy-start.4 = (bf16[64,2048]{1,0:T(8,128)(2,1)S(1)}, bf16[64,2048]{1,0:T(8,128)(2,1)}, u32[]{:S(2)}) copy-start(bf16[64,2048]{1,0:T(8,128)(2,1)} %param.22) | copy-start | bytes 786436
  102.8 68.9 %copy-start.5 = (bf16[64,2048]{1,0:T(8,128)(2,1)S(1)}, bf16[64,2048]{1,0:T(8,128)(2,1)}, u32[]{:S(2)}) copy-start(bf16[64,2048]{1,0:T(8,128)(2,1)} %param.21) | copy-start | bytes 786436
  102.8 8.1 collective-permute-start
  110.9 9.0 %collective-permute-start.1 = (f32[32,2048]{1,0:T(8,128)S(1)}, f32[32,2048]{1,0:T(8,128)S(1)}, u32[]{:S(2)}, u32[]{:S(2)}) collective-permute-start(f32[32,2048]{1,0:T(8,128)S(1)} %add.250), channel_id=1, source_target_pairs={{0,2},{1,3},{2,0},{3,1},{4,6},{5,7},{6,4},{7,5},{8,10},{9,11},{10,... | collective-permute-start | bytes 786440 | tf_op jit(solution)/shard_map/ppermute | solution.py:20
  121.1 710.2 %reduce-scatter.2.cloned.1.call-start = ((), (), s32[]{:S(2)}) async-start(), calls=%async_computation.3 | async-start | bytes 8454144 | tf_op jit(solution)/shard_map/reduce_scatter | solution.py:176
  179.6 653.6 %copy-start.7 = (f32[2048]{0:T(1024)S(1)}, f32[2048]{0:T(1024)}, u32[]{:S(2)}) copy-start(f32[2048]{0:T(1024)} %param.23) | copy-start | bytes 24580
Sparse Core Ops, SparseCore 0:
  121.2 46.8 all-gather.1
  179.8 651.4 reduce-scatter.1
